TPU v7x, 768 devices: a whole 4x8x12 slice. The times are simulated.
768 devices in a mesh: grid: 24 (over x_hi, z), ks: 32 (over x_lo, y, core).
Axes of the slice: x: 4 (x_hi: 2, x_lo: 2; x = x_hi * 2 + x_lo), y: 8, z: 12, core: 2. Of those that a mesh axis runs over, the one named last changes fastest.
Arguments:
- orbitals: bfloat16 [32, 256, 64, 24, 128], P('ks', None, None, 'grid'), may hold values from -2 to 2
- occupied: int32 [32], replicated, may hold values from 64 to 256, as said below
- kweight: int32 [32], replicated, may hold values from 1 to 8
Outputs:
- spin_density: float32 [2, 64, 24, 128], P(None, None, 'grid')
- potential: float32 [2, 64, 24, 128], P(None, None, 'grid')
- flux: float32 [2, 64, 3, 24, 128], P(None, None, None, 'grid')
Inputs may be any that keep to these rules, and one draw needn't show every extreme that they name: Some group has all 256 bands occupied.
All inputs are finite; a program needn't handle non-finite values.
Results may differ from a plain program's by a relative error of at most 0.0003.
Values sent between devices are 32-bit elements; how exact they have to be, the bound alone decides.
A program may use at most 32 MiB of HBM per device.

v0:
```python
import math

import jax
import jax.numpy as jnp
from jax import lax
from jax.sharding import PartitionSpec as P

BAND_BLOCK = 64


exchange_coef = 0.75 * (3.0 / math.pi) ** (1.0 / 3.0)
kappa_value = 0.804
mu_value = 0.2195
fermi_term = 4.0 * (3.0 * math.pi * math.pi) ** (2.0 / 3.0)


def partner_2(block, axis, stride):
    count = lax.axis_size(axis)
    route = []
    for low in range(count):
        high = low | 1 << stride
        if high != low and high < count:
            route += [(low, high), (high, low)]
    return lax.ppermute(block, axis, route)


def extended(cells, sides, width):
    for axis, dim in sides:
        count = lax.axis_size(axis)
        head = lax.slice_in_dim(cells, 0, width, axis=dim)
        tail = lax.slice_in_dim(cells, cells.shape[dim] - width, cells.shape[dim], axis=dim)
        cells = jnp.concatenate(
            [
                lax.ppermute(tail, axis, [(i, (i + 1) % count) for i in range(count)]),
                cells,
                lax.ppermute(head, axis, [((i + 1) % count, i) for i in range(count)]),
            ],
            axis=dim,
        )
    return cells


def energy_total(density, gradient):
    scaled = 2.0 * density
    square = 4.0 * jnp.sum(gradient * gradient, axis=2)
    reduced = square / (fermi_term * scaled ** (8.0 / 3.0))
    enhance = 1.0 + kappa_value - kappa_value / (1.0 + mu_value * reduced / kappa_value)
    exchange = -0.5 * exchange_coef * scaled ** (4.0 / 3.0) * enhance
    total = density[0] + density[1]
    polar = (density[0] - density[1]) / total
    radius = (3.0 / (4.0 * math.pi * total)) ** (1.0 / 3.0)
    correl = -total * 0.44 / (radius + 7.8) * (1.0 - 0.5 * polar * polar)
    return jnp.sum(exchange) + jnp.sum(correl)


def square_bands(flat, weight, count, trips):

    def add_block(step, total):
        start = step * BAND_BLOCK
        values = lax.dynamic_slice_in_dim(flat, start, BAND_BLOCK, 0).astype(jnp.float32)
        indices = start + jnp.arange(BAND_BLOCK, dtype=jnp.int32)
        factor = jnp.where(indices < count, weight, 0.0)
        return total + jnp.dot(factor, values * values, precision=lax.Precision.HIGHEST)

    return lax.fori_loop(0, trips, add_block, jnp.zeros((flat.shape[1],), jnp.float32))


def on_device(orbitals, occupied, kweight):
    group_index = lax.axis_index("ks")
    is_up = group_index % 2 == 0
    weights = kweight.astype(jnp.float32)
    up_total = jnp.sum(weights[0::2])
    down_total = jnp.sum(weights[1::2])
    my_weight = weights[group_index] / jnp.where(is_up, up_total, down_total)
    my_count = occupied[group_index]
    local = orbitals[0]
    bands, rows_y, planes, depth = local.shape
    flat = local.reshape(bands, rows_y * planes * depth)
    trips = bands // BAND_BLOCK
    partial_value = square_bands(flat, my_weight, my_count, trips).reshape(rows_y, planes, depth)
    upper = jnp.where(is_up, partial_value, 0.0)
    lower = jnp.where(is_up, 0.0, partial_value)
    owner_up = group_index < lax.axis_size("ks") // 2
    stacked = jnp.concatenate([upper, lower], axis=0)
    own_rows = lax.psum_scatter(stacked, "ks", scatter_dimension=0, tiled=True)
    bit_number = lax.axis_size("ks").bit_length() - 2
    partner = partner_2(own_rows, "ks", bit_number)
    both = jnp.stack(
        [jnp.where(owner_up, own_rows, partner), jnp.where(owner_up, partner, own_rows)]
    )
    padded = extended(both, (("grid", 2), ("ks", 1)), 1)
    center = padded[:, 1:-1, 1:-1]
    grad_y = (padded[:, 2:, 1:-1] - padded[:, :-2, 1:-1]) * 0.5
    grad_x = (padded[:, 1:-1, 2:] - padded[:, 1:-1, :-2]) * 0.5
    grad_z = (jnp.roll(center, -1, 3) - jnp.roll(center, 1, 3)) * 0.5
    gradient = jnp.stack([grad_y, grad_x, grad_z], axis=2)
    potential, flux = jax.grad(energy_total, argnums=(0, 1))(center, gradient)
    mine_potential = jnp.where(owner_up, potential[0], potential[1])
    mine_flux = jnp.where(owner_up, flux[0], flux[1])
    gathered = (
        lax.all_gather(own_rows, "ks", axis=0, tiled=True),
        lax.all_gather(mine_potential, "ks", axis=0, tiled=True),
        lax.all_gather(mine_flux, "ks", axis=0, tiled=True),
    )
    spin_density = gathered[0].reshape(2, rows_y, planes, depth)
    potential_out = gathered[1].reshape(2, rows_y, planes, depth)
    flux_out = gathered[2].reshape(2, rows_y, 3, planes, depth)
    return (spin_density, potential_out, flux_out)


def solution(mesh):
    placed = (P("ks", None, None, "grid", None), P(), P())
    return jax.shard_map(
        on_device,
        mesh=mesh,
        in_specs=placed,
        out_specs=(
            P(None, None, "grid", None),
            P(None, None, "grid", None),
            P(None, None, None, "grid", None),
        ),
        check_vma=False,
    )
```

profile of v0, /device:TPU:1, one launch (start us, length us, event | category | flops | bytes accessed | tf_op | source)
XLA Modules:
  0.0 382.2 jit_solution(16516886998583825978)
XLA Ops:
  7.2 0.7 convert_element_type.10
  7.9 0.1 slice.48
  8.0 0.1 slice.49
  8.1 0.6 reduce_sum.27
  8.7 0.7 reduce_sum.28
  9.4 0.6 dynamic_slice.14
  10.0 1.2 dynamic_slice.13
  11.2 12.3 %copy.31 = bf16[32,8,64,128]{3,1,2,0:T(8,128)(2,1)} copy(bf16[32,8,64,128]{3,2,1,0:T(8,128)(2,1)} %bitcast.89) | data formatting | bytes 8388608
  25.3 12.5 %while.14 = (s32[]{:T(128)}, f32[8192]{0:T(1024)S(1)}, s32[]{:T(128)}, f32[]{:T(128)}, bf16[256,8192]{1,0:T(8,128)(2,1)}, /*index=5*/s32[]{:T(128)}, s32[]{:T(128)}, s32[]{:T(128)}, s32[]{:T(128)}) while((s32[]{:T(128)}, f32[8192]{0:T(1024)S(1)}, s32[]{:T(128)}, f32[]{:T(128)}, bf16[256,8192]{1,0:T(8,128)(2,1)}, ...), condition=%wide.region_3.4_spmd.clone, body=%wide.region_2.3_spmd.clone.sunk | while | flops 7356615 | bytes 1180829 | solution.py:65
  25.4 3.1 fusion.41
  28.5 3.1 fusion.41
  31.6 3.1 fusion.41
  34.7 3.1 fusion.41
  37.8 0.6 pad_maximum_fusion
  38.5 1.3 dynamic-slice
  40.4 211.1 %all-reduce.7.cloned.1.call-done = f32[128,1,128]{2,0,1:T(8,128)} async-done(((f32[128,1,128]{2,0,1:T(8,128)}), f32[128,1,128]{2,0,1:T(8,128)}) %all-reduce.7.cloned.1.call-update) | async-done | bytes 65552
  251.6 0.7 constant_dynamic-slice_fusion
  252.2 1.9 collective-permute-start
  254.2 33.6 %all_gather.9 = f32[128,1,128]{2,1,0:T(1,128)S(1)} all-gather(f32[4,1,128]{2,1,0:T(1,128)S(1)} %bitcast.104), channel_id=1, replica_groups=mesh['grid'=24,'ks'=32] {'ks'}, dimensions={0}, use_global_device_ids=true | all-gather | bytes 67584 | tf_op jit(solution)/shard_map/all_gather | solution.py:101
  287.8 0.7 negate_bitcast_fusion
  288.5 3.3 collective-permute-start.1
  291.8 7.4 %collective-permute-start.2 = (f32[2,4,1,128]{3,1,0,2:T(4,128)S(1)}, f32[2,4,1,128]{3,1,0,2:T(4,128)S(1)}, u32[]{:S(2)}, u32[]{:S(2)}) collective-permute-start(f32[2,4,1,128]{3,1,0,2:T(4,128)S(1)} %fusion.29), channel_id=1, source_target_pairs={{32,0},{64,32},{96,64},{128,96},{160,128},{192,160},{224,192},{256... | collective-permute-start | bytes 12296 | tf_op jit(solution)/shard_map/ppermute | solution.py:36
  299.4 0.5 collective-permute-done.2
  299.9 2.9 collective-permute-start.3
  302.9 2.6 collective-permute-start.4
  305.5 0.1 fusion.22
  305.6 0.6 collective-permute-done.4
  306.4 34.4 %all-gather.1 = f32[1,128,3,1,128]{4,3,2,0,1:T(1,128)S(1)} all-gather(f32[1,4,3,1,128]{4,3,2,0,1:T(1,128)S(1)} %copy.24), channel_id=3, replica_groups=mesh['grid'=24,'ks'=32] {'ks'}, dimensions={1}, use_global_device_ids=true | all-gather | bytes 202752 | tf_op jit(solution)/shard_map/all_gather | solution.py:103
  340.9 32.5 %all-gather = f32[1,128,1,128]{3,2,0,1:T(1,128)S(1)} all-gather(f32[1,4,1,128]{3,2,0,1:T(1,128)S(1)} %bitcast.105), channel_id=2, replica_groups=mesh['grid'=24,'ks'=32] {'ks'}, dimensions={1}, use_global_device_ids=true | all-gather | bytes 67584 | tf_op jit(solution)/shard_map/all_gather | solution.py:102
  373.4 0.6 copy.42
  374.0 0.6 copy.43
  374.6 0.7 copy.44
  (24 shorter events, 0.4 us)
Async XLA Ops:
  7.2 244.4 %all-reduce.7.cloned.1.call-start = ((), (), s32[]{:S(2)}) async-start(), calls=%async_computation | async-start | bytes 131072
  252.2 35.6 %collective-permute-start = (f32[4,1,128]{2,0,1:T(4,128)S(1)}, f32[4,1,128]{2,0,1:T(4,128)S(1)}, u32[]{:S(2)}, u32[]{:S(2)}) collective-permute-start(f32[4,1,128]{2,0,1:T(4,128)S(1)} %constant_dynamic-slice_fusion), channel_id=1, source_target_pairs={{0,16},{16,0},{1,17},{17,1},{2,18},{18,2},{3,19},{19,3},{4,20},{20... | collective-permute-start | bytes 6152 | tf_op jit(solution)/shard_map/ppermute | solution.py:24
  288.5 10.9 %collective-permute-start.1 = (f32[2,4,1,128]{3,1,0,2:T(4,128)S(1)}, f32[2,4,1,128]{3,1,0,2:T(4,128)S(1)}, u32[]{:S(2)}, u32[]{:S(2)}) collective-permute-start(f32[2,4,1,128]{3,1,0,2:T(4,128)S(1)} %fusion.29), channel_id=1, source_target_pairs={{0,32},{32,64},{64,96},{96,128},{128,160},{160,192},{192,224},{224... | collective-permute-start | bytes 12296 | tf_op jit(solution)/shard_map/ppermute | solution.py:34
  291.8 8.1 %collective-permute-start.2 = (f32[2,4,1,128]{3,1,0,2:T(4,128)S(1)}, f32[2,4,1,128]{3,1,0,2:T(4,128)S(1)}, u32[]{:S(2)}, u32[]{:S(2)}) collective-permute-start(f32[2,4,1,128]{3,1,0,2:T(4,128)S(1)} %fusion.29), channel_id=1, source_target_pairs={{32,0},{64,32},{96,64},{128,96},{160,128},{192,160},{224,192},{256... | collective-permute-start | bytes 12296 | tf_op jit(solution)/shard_map/ppermute | solution.py:36
  299.9 5.7 %collective-permute-start.3 = (f32[2,1,3,128]{3,1,0,2:T(1,128)S(1)}, f32[2,1,3,128]{3,1,0,2:T(1,128)S(1)}, u32[]{:S(2)}, u32[]{:S(2)}) collective-permute-start(f32[2,1,3,128]{3,1,0,2:T(1,128)S(1)} %get-tuple-element.135), channel_id=1, source_target_pairs={{1,0},{2,1},{3,2},{4,3},{5,4},{6,5},{7,6},{8,7},{9,8},{10,9},{11,1... | collective-permute-start | bytes 9224 | tf_op jit(solution)/shard_map/ppermute | solution.py:36
  302.9 3.4 collective-permute-start.4
Sparse Core Ops, SparseCore 0:
  38.6 212.8 all-reduce.6
where the time goes:
time: 383 us; the launch traced here: 382 us
  waiting for transfers between devices  212 us (55%)
  blocking collectives  101 us (26%)
  starting transfers between devices  18.2 us (5%)
  local copies, waits for them, and re-layouts  18.2 us (5%)
  between operations  16.7 us (4%)
  matrix products  12.3 us (3%)
    unnamed x2, waiting for transfers between devices  211 us
    all_gather x1, blocking collectives, on_device(): lax.all_gather(mine_flux, 'ks', axis=0, tiled=True)  34.4 us
    all_gather x1, blocking collectives, on_device(): lax.all_gather(own_rows, 'ks', axis=0, tiled=True)  33.6 us
    all_gather x1, blocking collectives, on_device(): lax.all_gather(mine_potential, 'ks', axis=0, tiled=True)  32.5 us
    unnamed x6, local copies, waits for them, and re-layouts  16.2 us
    dot_general x4, matrix products, add_block(): jnp.dot(factor, values * values, precision=lax.Precision.HIGHEST)  12.3 us
    ppermute x2, starting transfers between devices, extended(): lax.ppermute(head, axis, [((i + 1) % count, i) for i in range(count)])  10.3 us
  transfers between devices with their start and end apart: 6, of which 3 were waited for; matrix products, arithmetic and copies ran while one was open for 0% of the time, Pallas kernels for 0%

commit v1 on v0

v1 whole, which is shorter than its diff:
```python
import functools
import math

import jax
import jax.numpy as jnp
from jax import lax
from jax.experimental import pallas as pl
from jax.experimental.pallas import tpu as pltpu
from jax.sharding import PartitionSpec as P

MESH = pl.DeviceIdType.MESH
CHUNKS = 8

exchange_coef = 0.75 * (3.0 / math.pi) ** (1.0 / 3.0)
kappa_value = 0.804
mu_value = 0.2195
fermi_term = 4.0 * (3.0 * math.pi * math.pi) ** (2.0 / 3.0)
radius_coef = (3.0 / (4.0 * math.pi)) ** (1.0 / 3.0)


def gather_kernel(
    sizes, orb_hbm, occ_hbm, kw_hbm, dens_ref, grad_ref,
    orb, occ, kw, part, recv, mine, halo, slope,
    load_sem, scalar_sem, rs_send, rs_recv, swap_send, swap_recv, halo_send, halo_recv, ag_send, ag_recv,
):
    n_grid, n_chip, n_y, n_z, bands = sizes
    n_x = n_chip // n_y
    g = lax.axis_index("grid")
    k = lax.axis_index("ks")
    core = k % 2
    chip = k // 2
    cx, cy = chip // n_y, chip % n_y
    block = bands // CHUNKS

    loads = [
        pltpu.make_async_copy(orb_hbm.at[pl.ds(i * block, block)], orb.at[pl.ds(i * block, block)], load_sem.at[i])
        for i in range(CHUNKS)
    ]
    scalars = [
        pltpu.make_async_copy(occ_hbm, occ, scalar_sem.at[0]),
        pltpu.make_async_copy(kw_hbm, kw, scalar_sem.at[1]),
    ]
    for copy in scalars + loads:
        copy.start()

    def shard_of(x, y, grid):
        return (x + grid // n_z) % n_x * n_y + y

    own = shard_of(cx, cy, g)

    steps = sorted(
        ((dx, dy) for dx in range(n_x) for dy in range(n_y) if dx or dy),
        key=lambda s: (-(s[0] + min(s[1], n_y - s[1])), s),
    )
    peers = []
    for dx, dy in steps:
        x, y = (cx + dx) % n_x, (cy + dy) % n_y
        peers.append(((x * n_y + y) * 2 + core, shard_of(x, y, g)))
    sides = []
    for d in (1, n_grid - 1):
        side = (g + d) % n_grid
        x = (own // n_y + side // n_z) % n_x
        sides.append((side, (x * n_y + cy) * 2))
    partner = chip * 2 + 1 - core

    barrier = pltpu.get_barrier_semaphore()
    for peer, _ in peers:
        pl.semaphore_signal(barrier, inc=1, device_id=(g, peer), device_id_type=MESH)
    for side, base in sides:
        for c in range(2):
            pl.semaphore_signal(barrier, inc=1, device_id=(side, base + c), device_id_type=MESH)
    pl.semaphore_signal(barrier, inc=1, device_id=(g, partner), device_id_type=MESH)

    for copy in scalars:
        copy.wait()
    count = occ[k]
    whole = kw[core]
    for i in range(1, kw.shape[0] // 2):
        whole = whole + kw[2 * i + core]
    shape = part.shape
    flat = (shape[0] * shape[1], shape[2])
    scale = jnp.full(flat, kw[k], jnp.int32).astype(jnp.float32) / jnp.full(flat, whole, jnp.int32).astype(jnp.float32)

    total = jnp.zeros(flat, jnp.float32)
    for i in range(CHUNKS):
        loads[i].wait()

        def add(b, acc):
            values = orb[b].astype(jnp.float32)
            return acc + jnp.where(b < count, values * values, 0.0)

        total = lax.fori_loop(i * block, (i + 1) * block, add, total, unroll=8)
    total = total * scale
    for j in range(shape[0]):
        part[j] = total[j * shape[1]:(j + 1) * shape[1]]

    pl.semaphore_wait(barrier, len(peers) + 5)

    def send(src, dst, send_sem, recv_sem, device):
        copy = pltpu.make_async_remote_copy(
            src_ref=src, dst_ref=dst, send_sem=send_sem, recv_sem=recv_sem, device_id=device, device_id_type=MESH
        )
        copy.start()
        return copy

    def wait_for(ref, sem):
        pltpu.make_async_copy(ref, ref, sem).wait()

    for i, (peer, shard) in enumerate(peers):
        send(part.at[shard], recv.at[i], rs_send, rs_recv, (g, peer))
    result = part[own]
    wait_for(recv, rs_recv)
    for i in range(len(peers)):
        result = result + recv[i]
    mine[core] = result

    for d, (side, base) in enumerate(sides):
        for c in range(2):
            send(mine.at[core], halo.at[1 - d, core], halo_send, halo_recv, (side, base + c))
    swap = send(mine.at[core], mine.at[core], swap_send, swap_recv, (g, partner))
    swap.wait()
    for peer, _ in peers:
        send(mine, dens_ref.at[:, own], ag_send.at[0], ag_recv.at[0], (g, peer))
    dens_ref[:, own] = mine[...]
    wait_for(halo, halo_recv)
    slope[...] = (halo[0] - halo[1]) * 0.5
    for peer, _ in peers:
        send(slope, grad_ref.at[:, own], ag_send.at[1], ag_recv.at[1], (g, peer))
    grad_ref[:, own] = slope[...]

    wait_for(recv, rs_send)
    wait_for(halo, halo_send)
    rest = pl.ds(0, len(peers))
    for i, ref in enumerate((dens_ref, grad_ref)):
        wait_for(ref.at[:, rest], ag_send.at[i])
        wait_for(ref.at[:, rest], ag_recv.at[i])


def energy_kernel(dens_ref, grad_ref, dens_out, pot_out, flux_out):
    rows, depth = dens_ref.shape[1:]
    up, down = dens_ref[0], dens_ref[1]
    dens_out[pl.ds(0, rows)] = up
    dens_out[pl.ds(rows, rows)] = down
    both = up + down
    polar = (up - down) / both
    radius = radius_coef * jnp.exp(jnp.log(both) * (-1.0 / 3.0))
    inverse = 1.0 / (radius + 7.8)
    front = -0.44 * inverse
    even = (1.0 - 0.5 * polar * polar) * (1.0 + radius * inverse * (1.0 / 3.0))
    for s, (value, sign) in enumerate(((up, 1.0), (down, -1.0))):
        scaled = 2.0 * value
        cube = jnp.exp(jnp.log(scaled) * (1.0 / 3.0))
        power = scaled * cube
        over = 1.0 / power
        grad_y = (pltpu.roll(value, rows - 1, 0) - pltpu.roll(value, 1, 0)) * 0.5
        grad_z = (pltpu.roll(value, depth - 1, 1) - pltpu.roll(value, 1, 1)) * 0.5
        grad_x = grad_ref[s]
        square = 4.0 * (grad_y * grad_y + grad_x * grad_x + grad_z * grad_z)
        reduced = square * over * over * (1.0 / fermi_term)
        ratio = 1.0 / (1.0 + (mu_value / kappa_value) * reduced)
        enhance = 1.0 + kappa_value - kappa_value * ratio
        slope = mu_value * ratio
        exchange = -exchange_coef * cube * (
            (4.0 / 3.0) * enhance - (8.0 / 3.0) * (reduced * ratio) * slope
        )
        pot_out[pl.ds(s * rows, rows)] = exchange + front * (even - polar * (sign - polar))
        factor = (-4.0 * exchange_coef / fermi_term) * (slope * ratio) * over
        for c, part in enumerate((grad_y, grad_x, grad_z)):
            flux_out[pl.ds(s * 3 * rows + c, rows, stride=3)] = factor * part


def on_device(n_grid, n_chip, n_y, n_z, orbitals, occupied, kweight):
    _, bands, rows, _, depth = orbitals.shape
    local = orbitals.reshape(bands, rows, depth)
    shard = rows // n_chip
    out = jax.ShapeDtypeStruct((2, n_chip, shard, depth), jnp.float32)
    vmem = pl.BlockSpec(memory_space=pltpu.VMEM)
    dma = pltpu.SemaphoreType.DMA
    dens, grad = pl.pallas_call(
        functools.partial(gather_kernel, (n_grid, n_chip, n_y, n_z, bands)),
        out_shape=(out, out),
        in_specs=[pl.BlockSpec(memory_space=pl.ANY)] * 3,
        out_specs=(vmem, vmem),
        scratch_shapes=[
            pltpu.VMEM((bands, rows, depth), jnp.bfloat16),
            pltpu.SMEM(occupied.shape, jnp.int32),
            pltpu.SMEM(kweight.shape, jnp.int32),
            pltpu.VMEM((n_chip, shard, depth), jnp.float32),
            pltpu.VMEM((n_chip - 1, shard, depth), jnp.float32),
            pltpu.VMEM((2, shard, depth), jnp.float32),
            pltpu.VMEM((2, 2, shard, depth), jnp.float32),
            pltpu.VMEM((2, shard, depth), jnp.float32),
            dma((CHUNKS,)),
            dma((2,)),
            dma(()),
            dma(()),
            dma(()),
            dma(()),
            dma(()),
            dma(()),
            dma((2,)),
            dma((2,)),
        ],
        compiler_params=pltpu.CompilerParams(collective_id=0, has_side_effects=True),
        name="density",
    )(local, occupied, kweight)
    dens, grad = dens.reshape(2, rows, depth), grad.reshape(2, rows, depth)
    flat = functools.partial(jax.ShapeDtypeStruct, dtype=jnp.float32)
    outs = pl.pallas_call(
        energy_kernel,
        out_shape=(flat((2 * rows, depth)), flat((2 * rows, depth)), flat((6 * rows, depth))),
        in_specs=[vmem, vmem],
        out_specs=(vmem, vmem, vmem),
        name="energy",
    )(dens, grad)
    return (
        outs[0].reshape(2, rows, 1, depth),
        outs[1].reshape(2, rows, 1, depth),
        outs[2].reshape(2, rows, 3, 1, depth),
    )


def solution(mesh):
    n_grid, n_ks = mesh.shape["grid"], mesh.shape["ks"]
    placed = (P("ks", None, None, "grid", None), P(), P())
    return jax.shard_map(
        functools.partial(on_device, n_grid, n_ks // 2, 8, 12),
        mesh=mesh,
        in_specs=placed,
        out_specs=(
            P(None, None, "grid", None),
            P(None, None, "grid", None),
            P(None, None, None, "grid", None),
        ),
        check_vma=False,
    )
```

time: 383 us -> 37 us (0.10)
  waiting for transfers between devices: 212 us -> 0 us
  blocking collectives: 101 us -> 0 us
  Pallas kernels: 0 us -> 36.2 us
  local copies, waits for them, and re-layouts: 18.2 us -> 0 us
  starting transfers between devices: 18.2 us -> 0 us
  between operations: 16.7 us -> 0.64 us
  matrix products: 12.3 us -> 0 us
    unnamed x2 -> x0, waiting for transfers between devices: 211 us -> none
    all_gather x3 -> x0, blocking collectives: 101 us -> none  [the longest x1 34.4 us: on_device(): lax.all_gather(mine_flux, 'ks', axis=0, tiled=True)]
    pallas_call x0 -> x2, Pallas kernels: none -> 36.2 us  [the longest x1 34.5 us: on_device(): pl.pallas_call(functools.partial(gather_kernel, (n_grid, n_chip, n_y, n_z...]
    ppermute x5 -> x0, starting transfers between devices: 18.1 us -> none  [the longest x2 10.3 us: extended(): lax.ppermute(head, axis, [((i + 1) % count, i) for i in range(count)])]
    unnamed x6 -> x0, local copies, waits for them, and re-layouts: 16.2 us -> none
    dot_general x4 -> x0, matrix products: 12.3 us -> none  [add_block(): jnp.dot(factor, values * values, precision=lax.Precision.HIGHEST)]
  transfers between devices with their start and end apart: 6 -> 0, of which waited for: 3 -> 0; matrix products, arithmetic and copies ran while one was open for 0% -> 0% of each run, Pallas kernels for 0% -> 0%
where the time goes in v1:
time: 37 us; the launch traced here: 36.9 us
  Pallas kernels  36.2 us (98%)
  between operations  0.64 us (2%)
    pallas_call x1, Pallas kernels, on_device(): pl.pallas_call(functools.partial(gather_kernel, (n_grid, n_chip, n_y, n_z...  34.5 us
    pallas_call x1, Pallas kernels, on_device(): pl.pallas_call(energy_kernel, out_shape=(flat((2 * rows, depth)), flat((2...  1.73 us

profile of v1, /device:TPU:1, one launch (start us, length us, event | category | flops | bytes accessed | tf_op | source)
XLA Modules:
  0.0 36.9 jit_solution(7426481854095484224)
XLA Ops:
  0.6 34.5 %density.1 = (f32[2,16,4,128]{3,2,1,0:T(4,128)}, f32[2,16,4,128]{3,2,1,0:T(4,128)}) custom-call(bf16[256,64,128]{2,1,0:T(8,128)(2,1)} %bitcast.10, s32[32]{0:T(128)} %occ_hbm.1, s32[32]{0:T(128)} %kw_hbm.1), custom_call_target="tpu_custom_call" | custom-call | tf_op jit(solution)/shard_map/density/pallas_call | solution.py:179
  35.1 1.7 %energy.1 = (f32[128,128]{1,0:T(8,128)}, f32[128,128]{1,0:T(8,128)}, f32[384,128]{1,0:T(8,128)}) custom-call(f32[2,64,128]{2,1,0:T(8,128)} %bitcast.11, f32[2,64,128]{2,1,0:T(8,128)} %bitcast.12), custom_call_target="tpu_custom_call" | custom-call | tf_op jit(solution)/shard_map/energy/pallas_call | solution.py:209

commit v2 on v1

v2 whole, which is shorter than its diff:
```python
import functools
import math

import jax
import jax.numpy as jnp
from jax import lax
from jax.experimental import pallas as pl
from jax.experimental.pallas import tpu as pltpu
from jax.sharding import PartitionSpec as P

MESH = pl.DeviceIdType.MESH
CHUNKS = 4
UNROLL = 8
VMEM_LIMIT = 62 << 20

exchange_coef = 0.75 * (3.0 / math.pi) ** (1.0 / 3.0)
kappa_value = 0.804
mu_value = 0.2195
fermi_term = 4.0 * (3.0 * math.pi * math.pi) ** (2.0 / 3.0)
radius_coef = (3.0 / (4.0 * math.pi)) ** (1.0 / 3.0)


def gather_kernel(
    sizes, orb_hbm, occ_hbm, kw_hbm, dens_ref, grad_ref,
    orb, occ, kw, part, recv, mine,
    load_sem, scalar_sem, rs_send, rs_recv, reply_send, reply_recv, ag_send, ag_recv, known,
):
    n_grid, n_x, n_y, n_z = sizes
    bands, rows = orb_hbm.shape[:2]
    g = lax.axis_index("grid")
    k = lax.axis_index("ks")
    core = k % 2
    chip = k // 2
    cx, cy = chip // n_y, chip % n_y
    z = g % n_z
    first, last = z == 0, z == n_z - 1
    after, before = (g + 1) % n_grid, (g + n_grid - 1) % n_grid
    tile = rows // n_y
    thick = rows // CHUNKS
    tiles = n_y // CHUNKS
    FROM_AFTER, FROM_OWN, FROM_BEFORE = 0, 1, 2
    OWN, NEXT, PREVIOUS, SLOPE = 0, 1, 2, 3

    turns = sorted(range(CHUNKS), key=lambda m: -min(m, CHUNKS - m))
    chunks = [(cy // tiles + m) % CHUNKS for m in turns]
    loads = [
        pltpu.make_async_copy(
            orb_hbm.at[:, pl.ds(pl.multiple_of(m * thick, thick), thick)], orb.at[i], load_sem.at[i]
        )
        for i, m in enumerate(chunks)
    ]
    scalars = [
        pltpu.make_async_copy(occ_hbm, occ, scalar_sem.at[0]),
        pltpu.make_async_copy(kw_hbm, kw, scalar_sem.at[1]),
    ]
    for copy in loads[:1] + scalars + loads[1:]:
        copy.start()

    def index(x, y, c):
        return ((x % n_x) * n_y + y % n_y) * 2 + c

    partner = index(cx, cy, 1 - core)
    column = [
        (dy, c) for dy in sorted(range(n_y), key=lambda d: -min(d, n_y - d)) for c in range(2) if dy or c
    ]
    barrier = pltpu.get_barrier_semaphore()

    def greet(grid, peer):
        pl.semaphore_signal(barrier, inc=1, device_id=(grid, peer), device_id_type=MESH)

    @pl.when(first)
    def _():
        for dx in range(n_x):
            for dy in range(n_y):
                greet(before, index(cx + dx, cy + dy, core))
        for dy, c in column:
            greet(g, index(cx, cy + dy, (core + c) % 2))
        for dy in range(n_y):
            greet(g, index(cx + 1, cy + dy, core))

    @pl.when(z > 0)
    def _():
        greet(g, partner)

    @pl.when(z < n_z - 1)
    def _():
        for dx in range(n_x):
            for dy in range(n_y):
                greet(after, index(cx + dx, cy + dy, core))

    for copy in scalars:
        copy.wait()
    count = occ[k]
    whole = kw[core]
    for i in range(1, kw.shape[0] // 2):
        whole = whole + kw[2 * i + core]
    shape = (thick, mine.shape[2])
    scale = jnp.full(shape, kw[k], jnp.int32).astype(jnp.float32) / jnp.full(shape, whole, jnp.int32).astype(jnp.float32)

    def send(src, dst, send_sem, recv_sem, device):
        copy = pltpu.make_async_remote_copy(
            src_ref=src, dst_ref=dst, send_sem=send_sem, recv_sem=recv_sem, device_id=device, device_id_type=MESH
        )
        copy.start()

    def wait_for(ref, sem):
        pltpu.make_async_copy(ref, ref, sem).wait()

    target = jnp.where(first, g, before)
    source = jnp.where(first, FROM_OWN, FROM_AFTER)
    lanes = 4
    for i, m in enumerate(chunks):
        loads[i].wait()

        def add(step, sums):
            out = list(sums)
            for j in range(UNROLL):
                b = step * UNROLL + j
                values = orb[i, b].astype(jnp.float32)
                out[j % lanes] = out[j % lanes] + jnp.where(b < count, values * values, 0.0)
            return tuple(out)

        sums = lax.fori_loop(0, bands // UNROLL, add, (jnp.zeros(shape, jnp.float32),) * lanes)
        total = ((sums[0] + sums[1]) + (sums[2] + sums[3])) * scale
        for j in range(tiles):
            part[m * tiles + j] = total[j * tile:(j + 1) * tile]
        if i == 0:
            pl.semaphore_wait(
                barrier, jnp.where(first, 3 * n_y - 1, jnp.where(last, 2 * n_x * n_y + 1, n_x * n_y + 1))
            )

        @pl.when(last)
        def _():
            for j in range(tiles):
                to = m * tiles + j
                slot = (to - cy + n_y) % n_y
                for dx in range(n_x):
                    send(
                        part.at[to], recv.at[FROM_BEFORE, dx * n_y + slot], rs_send, rs_recv.at[FROM_BEFORE],
                        (after, index(cx + dx, to, core)),
                    )

        for j in range(tiles):
            to = m * tiles + j
            slot = (to - cy + n_y) % n_y
            send(
                part.at[to], recv.at[source, n_y + slot], rs_send, rs_recv.at[source],
                (target, index(cx + 1, to, core)),
            )

            @pl.when((z > 0) | (to != cy))
            def _():
                send(
                    part.at[to], recv.at[source, slot], rs_send, rs_recv.at[source],
                    (target, index(cx, to, core)),
                )

    whole_set = pl.ds(0, n_x * n_y)
    others = pl.ds(1, n_x * n_y - 1)

    def add_up(which, value):
        for i in range(1, n_x * n_y):
            value = value + recv[which, i]
        return value

    def reply(which, src, dst, grid, x):
        send(
            mine.at[src], mine.at[dst], reply_send.at[which], reply_recv.at[which], (grid, index(x, cy, core))
        )

    def spread(i, src, ref):
        for dy, c in column:
            send(mine.at[src], ref.at[core, cy], ag_send.at[i], ag_recv.at[i], (g, index(cx, cy + dy, (core + c) % 2)))
        ref[core, cy] = mine[src]

    @pl.when(z < n_z - 1)
    def _():
        wait_for(recv.at[FROM_AFTER, whole_set], rs_recv.at[FROM_AFTER])
        mine[NEXT] = add_up(FROM_AFTER, recv[FROM_AFTER, 0])
        reply(0, NEXT, OWN, after, cx)

    @pl.when(first)
    def _():
        wait_for(recv.at[FROM_OWN, others], rs_recv.at[FROM_OWN])
        mine[OWN] = add_up(FROM_OWN, part[cy])

    @pl.when(z > 0)
    def _():
        wait_for(mine.at[OWN], reply_recv.at[0])

    pl.semaphore_signal(known, inc=1, device_id=(g, partner), device_id_type=MESH)

    @pl.when(z < n_z - 1)
    def _():
        reply(1, OWN, PREVIOUS, after, cx)

    pl.semaphore_wait(known, 1)
    spread(0, OWN, dens_ref)

    @pl.when(last)
    def _():
        wait_for(mine.at[NEXT], reply_recv.at[2])

    @pl.when(first)
    def _():
        wait_for(recv.at[FROM_BEFORE, whole_set], rs_recv.at[FROM_BEFORE])
        mine[PREVIOUS] = add_up(FROM_BEFORE, recv[FROM_BEFORE, 0])

    @pl.when(z > 0)
    def _():
        wait_for(mine.at[PREVIOUS], reply_recv.at[1])

    mine[SLOPE] = (mine[NEXT] - mine[PREVIOUS]) * 0.5
    spread(1, SLOPE, grad_ref)

    @pl.when(first)
    def _():
        reply(2, OWN, NEXT, before, cx + 1)
        wait_for(mine.at[OWN], reply_send.at[2])
        wait_for(recv.at[FROM_OWN, others], rs_send)

    @pl.when(z < n_z - 1)
    def _():
        wait_for(mine.at[OWN], reply_send.at[0])
        wait_for(mine.at[OWN], reply_send.at[1])

    @pl.when(z > 0)
    def _():
        wait_for(recv.at[FROM_OWN, whole_set], rs_send)

    @pl.when(last)
    def _():
        wait_for(recv.at[FROM_OWN, whole_set], rs_send)

    for i in range(2):
        wait_for(recv.at[FROM_OWN, others], ag_send.at[i])
        wait_for(recv.at[FROM_OWN, others], ag_recv.at[i])


def energy_kernel(dens_ref, grad_ref, dens_out, pot_out, flux_out):
    rows, depth = dens_ref.shape[1:]
    up, down = dens_ref[0], dens_ref[1]
    dens_out[pl.ds(0, rows)] = up
    dens_out[pl.ds(rows, rows)] = down
    both = up + down
    polar = (up - down) / both
    radius = radius_coef * jnp.exp(jnp.log(both) * (-1.0 / 3.0))
    inverse = 1.0 / (radius + 7.8)
    front = -0.44 * inverse
    even = (1.0 - 0.5 * polar * polar) * (1.0 + radius * inverse * (1.0 / 3.0))
    for s, (value, sign) in enumerate(((up, 1.0), (down, -1.0))):
        scaled = 2.0 * value
        cube = jnp.exp(jnp.log(scaled) * (1.0 / 3.0))
        power = scaled * cube
        over = 1.0 / power
        grad_y = (pltpu.roll(value, rows - 1, 0) - pltpu.roll(value, 1, 0)) * 0.5
        grad_z = (pltpu.roll(value, depth - 1, 1) - pltpu.roll(value, 1, 1)) * 0.5
        grad_x = grad_ref[s]
        square = 4.0 * (grad_y * grad_y + grad_x * grad_x + grad_z * grad_z)
        reduced = square * over * over * (1.0 / fermi_term)
        ratio = 1.0 / (1.0 + (mu_value / kappa_value) * reduced)
        enhance = 1.0 + kappa_value - kappa_value * ratio
        slope = mu_value * ratio
        exchange = -exchange_coef * cube * (
            (4.0 / 3.0) * enhance - (8.0 / 3.0) * (reduced * ratio) * slope
        )
        pot_out[pl.ds(s * rows, rows)] = exchange + front * (even - polar * (sign - polar))
        factor = (-4.0 * exchange_coef / fermi_term) * (slope * ratio) * over
        for c, part in enumerate((grad_y, grad_x, grad_z)):
            flux_out[pl.ds(s * 3 * rows + c, rows, stride=3)] = factor * part


def on_device(n_grid, n_x, n_y, n_z, orbitals, occupied, kweight):
    _, bands, rows, _, depth = orbitals.shape
    local = orbitals.reshape(bands, rows, depth)
    tile = rows // n_y
    out = pltpu.VMEM((2, n_y, tile, depth), jnp.float32)
    vmem = pl.BlockSpec(memory_space=pltpu.VMEM)
    dma = pltpu.SemaphoreType.DMA
    dens, grad = pl.pallas_call(
        functools.partial(gather_kernel, (n_grid, n_x, n_y, n_z)),
        out_shape=(out, out),
        in_specs=[pl.BlockSpec(memory_space=pl.ANY)] * 3,
        out_specs=(vmem, vmem),
        scratch_shapes=[
            pltpu.VMEM((CHUNKS, bands, rows // CHUNKS, depth), jnp.bfloat16),
            pltpu.SMEM(occupied.shape, jnp.int32),
            pltpu.SMEM(kweight.shape, jnp.int32),
            pltpu.VMEM((n_y, tile, depth), jnp.float32),
            pltpu.VMEM((3, 2 * n_y, tile, depth), jnp.float32),
            pltpu.VMEM((4, tile, depth), jnp.float32),
            dma((CHUNKS,)),
            dma((2,)),
            dma(()),
            dma((3,)),
            dma((3,)),
            dma((3,)),
            dma((2,)),
            dma((2,)),
            pltpu.SemaphoreType.REGULAR,
        ],
        compiler_params=pltpu.CompilerParams(
            collective_id=0, has_side_effects=True, vmem_limit_bytes=VMEM_LIMIT
        ),
        name="density",
    )(local, occupied, kweight)
    dens, grad = dens.reshape(2, rows, depth), grad.reshape(2, rows, depth)
    flat = functools.partial(jax.ShapeDtypeStruct, dtype=jnp.float32)
    outs = pl.pallas_call(
        energy_kernel,
        out_shape=(flat((2 * rows, depth)), flat((2 * rows, depth)), flat((6 * rows, depth))),
        in_specs=[vmem, vmem],
        out_specs=(vmem, vmem, vmem),
        compiler_params=pltpu.CompilerParams(vmem_limit_bytes=8 << 20),
        name="energy",
    )(dens, grad)
    return (
        outs[0].reshape(2, rows, 1, depth),
        outs[1].reshape(2, rows, 1, depth),
        outs[2].reshape(2, rows, 3, 1, depth),
    )


def solution(mesh):
    n_grid, n_ks = mesh.shape["grid"], mesh.shape["ks"]
    placed = (P("ks", None, None, "grid", None), P(), P())
    return jax.shard_map(
        functools.partial(on_device, n_grid, 2, n_ks // 4, n_grid // 2),
        mesh=mesh,
        in_specs=placed,
        out_specs=(
            P(None, None, "grid", None),
            P(None, None, "grid", None),
            P(None, None, None, "grid", None),
        ),
        check_vma=False,
    )
```

time: 37 us -> 34.1 us (0.922)
  Pallas kernels: 36.2 us -> 33.3 us
    pallas_call x1, Pallas kernels: 34.5 us -> 32.5 us  [on_device(): pl.pallas_call(functools.partial(gather_kernel, (n_grid, n_x, n_y, n_z)),...]
    pallas_call x1, Pallas kernels: 1.73 us -> 0.85 us  [on_device(): pl.pallas_call(energy_kernel, out_shape=(flat((2 * rows, depth)), flat((2...]
where the time goes in v2:
time: 34.1 us; the launch traced here: 34 us
  Pallas kernels  33.3 us (98%)
  between operations  0.64 us (2%)
    pallas_call x1, Pallas kernels, on_device(): pl.pallas_call(functools.partial(gather_kernel, (n_grid, n_x, n_y, n_z)),...  32.5 us
    pallas_call x1, Pallas kernels, on_device(): pl.pallas_call(energy_kernel, out_shape=(flat((2 * rows, depth)), flat((2...  0.85 us

profile of v2, /device:TPU:1, one launch (start us, length us, event | category | flops | bytes accessed | tf_op | source)
XLA Modules:
  0.0 34.0 jit_solution(15378858016956362055)
XLA Ops:
  0.6 32.5 %density.1 = (f32[2,8,8,128]{3,2,1,0:T(8,128)S(1)}, f32[2,8,8,128]{3,2,1,0:T(8,128)S(1)}) custom-call(bf16[256,64,128]{2,1,0:T(8,128)(2,1)} %bitcast.12, s32[32]{0:T(128)} %occ_hbm.1, s32[32]{0:T(128)} %kw_hbm.1), custom_call_target="tpu_custom_call" | custom-call | tf_op jit(solution)/shard_map/density/pallas_call | solution.py:280
  33.1 0.9 %energy.1 = (f32[128,128]{1,0:T(8,128)}, f32[128,128]{1,0:T(8,128)}, f32[384,128]{1,0:T(8,128)}) custom-call(f32[2,64,128]{2,1,0:T(8,128)S(1)} %bitcast.10, f32[2,64,128]{2,1,0:T(8,128)S(1)} %bitcast.11), custom_call_target="tpu_custom_call" | custom-call | tf_op jit(solution)/shard_map/energy/pallas_call | solution.py:309

commit v3 on v2

--- a/solution.py
+++ b/solution.py
@@ -22,9 +22,13 @@
 
 def gather_kernel(
     sizes, orb_hbm, occ_hbm, kw_hbm, dens_ref, grad_ref,
-    orb, occ, kw, part, recv, mine,
-    load_sem, scalar_sem, rs_send, rs_recv, reply_send, reply_recv, ag_send, ag_recv, known,
+    *scratch,
 ):
+    orb = scratch[:CHUNKS]
+    (
+        occ, kw, part, recv, mine,
+        load_sem, scalar_sem, rs_send, rs_recv, reply_send, reply_recv, ag_send, ag_recv, known,
+    ) = scratch[CHUNKS:]
     n_grid, n_x, n_y, n_z = sizes
     bands, rows = orb_hbm.shape[:2]
     g = lax.axis_index("grid")
@@ -45,7 +49,7 @@
     chunks = [(cy // tiles + m) % CHUNKS for m in turns]
     loads = [
         pltpu.make_async_copy(
-            orb_hbm.at[:, pl.ds(pl.multiple_of(m * thick, thick), thick)], orb.at[i], load_sem.at[i]
+            orb_hbm.at[:, pl.ds(pl.multiple_of(m * thick, thick), thick)], orb[i], load_sem.at[i]
         )
         for i, m in enumerate(chunks)
     ]
@@ -82,11 +86,15 @@
     def _():
         greet(g, partner)
 
-    @pl.when(z < n_z - 1)
+    @pl.when(z < n_z - 2)
     def _():
         for dx in range(n_x):
             for dy in range(n_y):
                 greet(after, index(cx + dx, cy + dy, core))
+
+    @pl.when(z == n_z - 2)
+    def _():
+        greet(after, k)
 
     for copy in scalars:
         copy.wait()
@@ -106,39 +114,34 @@
     def wait_for(ref, sem):
         pltpu.make_async_copy(ref, ref, sem).wait()
 
-    target = jnp.where(first, g, before)
-    source = jnp.where(first, FROM_OWN, FROM_AFTER)
-    lanes = 4
+    target = jnp.where(first, g, jnp.where(last, after, before))
+    source = jnp.where(first, FROM_OWN, jnp.where(last, FROM_BEFORE, FROM_AFTER))
+    groups = count // UNROLL
+    rest = jnp.minimum(groups * UNROLL, bands - UNROLL)
+
+    def pair_sum(values):
+        while len(values) > 1:
+            values = [a + b for a, b in zip(values[::2], values[1::2])]
+        return values[0]
+
     for i, m in enumerate(chunks):
         loads[i].wait()
 
         def add(step, sums):
-            out = list(sums)
-            for j in range(UNROLL):
-                b = step * UNROLL + j
-                values = orb[i, b].astype(jnp.float32)
-                out[j % lanes] = out[j % lanes] + jnp.where(b < count, values * values, 0.0)
-            return tuple(out)
-
-        sums = lax.fori_loop(0, bands // UNROLL, add, (jnp.zeros(shape, jnp.float32),) * lanes)
-        total = ((sums[0] + sums[1]) + (sums[2] + sums[3])) * scale
+            values = [orb[i][step * UNROLL + j].astype(jnp.float32) for j in range(UNROLL)]
+            group = pair_sum([v * v for v in values])
+            return sums + jnp.where(step < groups, group, 0.0)
+
+        total = lax.fori_loop(0, bands // UNROLL, add, jnp.zeros(shape, jnp.float32), unroll=2)
+        values = [orb[i][rest + j].astype(jnp.float32) for j in range(UNROLL)]
+        total = total + pair_sum([jnp.where(groups * UNROLL + j < count, v * v, 0.0) for j, v in enumerate(values)])
+        total = total * scale
         for j in range(tiles):
             part[m * tiles + j] = total[j * tile:(j + 1) * tile]
         if i == 0:
             pl.semaphore_wait(
-                barrier, jnp.where(first, 3 * n_y - 1, jnp.where(last, 2 * n_x * n_y + 1, n_x * n_y + 1))
+                barrier, jnp.where(first, 3 * n_y - 1, jnp.where(last, n_x * n_y + 2, n_x * n_y + 1))
             )
-
-        @pl.when(last)
-        def _():
-            for j in range(tiles):
-                to = m * tiles + j
-                slot = (to - cy + n_y) % n_y
-                for dx in range(n_x):
-                    send(
-                        part.at[to], recv.at[FROM_BEFORE, dx * n_y + slot], rs_send, rs_recv.at[FROM_BEFORE],
-                        (after, index(cx + dx, to, core)),
-                    )
 
         for j in range(tiles):
             to = m * tiles + j
@@ -163,9 +166,9 @@
             value = value + recv[which, i]
         return value
 
-    def reply(which, src, dst, grid, x):
+    def reply(which, what, src, dst, grid, x):
         send(
-            mine.at[src], mine.at[dst], reply_send.at[which], reply_recv.at[which], (grid, index(x, cy, core))
+            mine.at[src], mine.at[dst], reply_send.at[which], reply_recv.at[what], (grid, index(x, cy, core))
         )
 
     def spread(i, src, ref):
@@ -173,11 +176,11 @@
             send(mine.at[src], ref.at[core, cy], ag_send.at[i], ag_recv.at[i], (g, index(cx, cy + dy, (core + c) % 2)))
         ref[core, cy] = mine[src]
 
-    @pl.when(z < n_z - 1)
+    @pl.when(z < n_z - 2)
     def _():
         wait_for(recv.at[FROM_AFTER, whole_set], rs_recv.at[FROM_AFTER])
         mine[NEXT] = add_up(FROM_AFTER, recv[FROM_AFTER, 0])
-        reply(0, NEXT, OWN, after, cx)
+        reply(0, 0, NEXT, OWN, after, cx)
 
     @pl.when(first)
     def _():
@@ -190,16 +193,24 @@
 
     pl.semaphore_signal(known, inc=1, device_id=(g, partner), device_id_type=MESH)
 
-    @pl.when(z < n_z - 1)
-    def _():
-        reply(1, OWN, PREVIOUS, after, cx)
+    @pl.when(z < n_z - 2)
+    def _():
+        reply(1, 1, OWN, PREVIOUS, after, cx)
+
+    @pl.when(last)
+    def _():
+        reply(2, 2, OWN, NEXT, before, cx)
 
     pl.semaphore_wait(known, 1)
     spread(0, OWN, dens_ref)
 
-    @pl.when(last)
+    @pl.when(z >= n_z - 2)
     def _():
         wait_for(mine.at[NEXT], reply_recv.at[2])
+
+    @pl.when(z == n_z - 2)
+    def _():
+        reply(1, 1, OWN, PREVIOUS, after, cx)
 
     @pl.when(first)
     def _():
@@ -215,20 +226,24 @@
 
     @pl.when(first)
     def _():
-        reply(2, OWN, NEXT, before, cx + 1)
+        reply(3, 0, PREVIOUS, OWN, before, cx + 1)
+        reply(2, 2, OWN, NEXT, before, cx + 1)
+        wait_for(mine.at[OWN], reply_send.at[3])
+        wait_for(recv.at[FROM_OWN, others], rs_send)
+
+    @pl.when(first | last)
+    def _():
         wait_for(mine.at[OWN], reply_send.at[2])
-        wait_for(recv.at[FROM_OWN, others], rs_send)
+
+    @pl.when(z < n_z - 2)
+    def _():
+        wait_for(mine.at[OWN], reply_send.at[0])
 
     @pl.when(z < n_z - 1)
     def _():
-        wait_for(mine.at[OWN], reply_send.at[0])
         wait_for(mine.at[OWN], reply_send.at[1])
 
     @pl.when(z > 0)
-    def _():
-        wait_for(recv.at[FROM_OWN, whole_set], rs_send)
-
-    @pl.when(last)
     def _():
         wait_for(recv.at[FROM_OWN, whole_set], rs_send)
 
@@ -283,7 +298,7 @@
         in_specs=[pl.BlockSpec(memory_space=pl.ANY)] * 3,
         out_specs=(vmem, vmem),
         scratch_shapes=[
-            pltpu.VMEM((CHUNKS, bands, rows // CHUNKS, depth), jnp.bfloat16),
+            *[pltpu.VMEM((bands, rows // CHUNKS, depth), jnp.bfloat16) for _ in range(CHUNKS)],
             pltpu.SMEM(occupied.shape, jnp.int32),
             pltpu.SMEM(kweight.shape, jnp.int32),
             pltpu.VMEM((n_y, tile, depth), jnp.float32),
@@ -293,7 +308,7 @@
             dma((2,)),
             dma(()),
             dma((3,)),
-            dma((3,)),
+            dma((4,)),
             dma((3,)),
             dma((2,)),
             dma((2,)),

time: 34.1 us -> 30.6 us (0.90)
  Pallas kernels: 33.3 us -> 29.8 us
    pallas_call x1, Pallas kernels: 32.5 us -> 29 us  [on_device(): pl.pallas_call(functools.partial(gather_kernel, (n_grid, n_x, n_y, n_z)),...]
where the time goes in v3:
time: 30.6 us; the launch traced here: 30.5 us
  Pallas kernels  29.8 us (97%)
  between operations  0.64 us (2%)
    pallas_call x1, Pallas kernels, on_device(): pl.pallas_call(functools.partial(gather_kernel, (n_grid, n_x, n_y, n_z)),...  29 us
    pallas_call x1, Pallas kernels, on_device(): pl.pallas_call(energy_kernel, out_shape=(flat((2 * rows, depth)), flat((2...  0.85 us

profile of v3, /device:TPU:1, one launch (start us, length us, event | category | flops | bytes accessed | tf_op | source)
XLA Modules:
  0.0 30.5 jit_solution(13771086601769512588)
XLA Ops:
  0.6 29.0 %density.1 = (f32[2,8,8,128]{3,2,1,0:T(8,128)S(1)}, f32[2,8,8,128]{3,2,1,0:T(8,128)S(1)}) custom-call(bf16[256,64,128]{2,1,0:T(8,128)(2,1)} %bitcast.12, s32[32]{0:T(128)} %occ_hbm.1, s32[32]{0:T(128)} %kw_hbm.1), custom_call_target="tpu_custom_call" | custom-call | tf_op jit(solution)/shard_map/density/pallas_call | solution.py:295
  29.6 0.9 %energy.1 = (f32[128,128]{1,0:T(8,128)}, f32[128,128]{1,0:T(8,128)}, f32[384,128]{1,0:T(8,128)}) custom-call(f32[2,64,128]{2,1,0:T(8,128)S(1)} %bitcast.10, f32[2,64,128]{2,1,0:T(8,128)S(1)} %bitcast.11), custom_call_target="tpu_custom_call" | custom-call | tf_op jit(solution)/shard_map/energy/pallas_call | solution.py:324

commit v4 on v3

--- a/solution.py
+++ b/solution.py
@@ -11,6 +11,7 @@
 MESH = pl.DeviceIdType.MESH
 CHUNKS = 4
 UNROLL = 8
+PARTS = 2
 VMEM_LIMIT = 62 << 20
 
 exchange_coef = 0.75 * (3.0 / math.pi) ** (1.0 / 3.0)
@@ -21,12 +22,12 @@
 
 
 def gather_kernel(
-    sizes, orb_hbm, occ_hbm, kw_hbm, dens_ref, grad_ref,
+    sizes, orb_hbm, occ_hbm, kw_hbm, dens_ref, pot_ref, flux_ref,
     *scratch,
 ):
     orb = scratch[:CHUNKS]
     (
-        occ, kw, part, recv, mine,
+        occ, kw, part, recv, mine, grad_ref, ready,
         load_sem, scalar_sem, rs_send, rs_recv, reply_send, reply_recv, ag_send, ag_recv, known,
     ) = scratch[CHUNKS:]
     n_grid, n_x, n_y, n_z = sizes
@@ -47,11 +48,15 @@
 
     turns = sorted(range(CHUNKS), key=lambda m: -min(m, CHUNKS - m))
     chunks = [(cy // tiles + m) % CHUNKS for m in turns]
+    half = bands // PARTS
     loads = [
         pltpu.make_async_copy(
-            orb_hbm.at[:, pl.ds(pl.multiple_of(m * thick, thick), thick)], orb[i], load_sem.at[i]
+            orb_hbm.at[pl.ds(p * half, half), pl.ds(pl.multiple_of(m * thick, thick), thick)],
+            orb[i].at[pl.ds(p * half, half)],
+            load_sem.at[i * PARTS + p],
         )
         for i, m in enumerate(chunks)
+        for p in range(PARTS)
     ]
     scalars = [
         pltpu.make_async_copy(occ_hbm, occ, scalar_sem.at[0]),
@@ -61,12 +66,19 @@
         copy.start()
 
     def index(x, y, c):
-        return ((x % n_x) * n_y + y % n_y) * 2 + c
+        return (lax.rem(x, n_x) * n_y + lax.rem(y, n_y)) * 2 + c
 
     partner = index(cx, cy, 1 - core)
     column = [
         (dy, c) for dy in sorted(range(n_y), key=lambda d: -min(d, n_y - d)) for c in range(2) if dy or c
     ]
+    gather_to = [index(cx, cy + dy, lax.rem(core + c, 2)) for dy, c in column]
+    rows_to = []
+    for m in chunks:
+        for j in range(tiles):
+            to = m * tiles + j
+            slot = lax.rem(to - cy + n_y, n_y)
+            rows_to.append((to, slot, index(cx + 1, to, core), index(cx, to, core)))
     barrier = pltpu.get_barrier_semaphore()
 
     def greet(grid, peer):
@@ -125,14 +137,16 @@
         return values[0]
 
     for i, m in enumerate(chunks):
-        loads[i].wait()
 
         def add(step, sums):
             values = [orb[i][step * UNROLL + j].astype(jnp.float32) for j in range(UNROLL)]
             group = pair_sum([v * v for v in values])
             return sums + jnp.where(step < groups, group, 0.0)
 
-        total = lax.fori_loop(0, bands // UNROLL, add, jnp.zeros(shape, jnp.float32), unroll=2)
+        total = jnp.zeros(shape, jnp.float32)
+        for p in range(PARTS):
+            loads[i * PARTS + p].wait()
+            total = lax.fori_loop(p * half // UNROLL, (p + 1) * half // UNROLL, add, total, unroll=2)
         values = [orb[i][rest + j].astype(jnp.float32) for j in range(UNROLL)]
         total = total + pair_sum([jnp.where(groups * UNROLL + j < count, v * v, 0.0) for j, v in enumerate(values)])
         total = total * scale
@@ -143,28 +157,23 @@
                 barrier, jnp.where(first, 3 * n_y - 1, jnp.where(last, n_x * n_y + 2, n_x * n_y + 1))
             )
 
-        for j in range(tiles):
-            to = m * tiles + j
-            slot = (to - cy + n_y) % n_y
+        for to, slot, across, along in rows_to[i * tiles:(i + 1) * tiles]:
             send(
-                part.at[to], recv.at[source, n_y + slot], rs_send, rs_recv.at[source],
-                (target, index(cx + 1, to, core)),
+                part.at[to], recv.at[source, n_y + slot], rs_send, rs_recv.at[source], (target, across)
             )
 
             @pl.when((z > 0) | (to != cy))
             def _():
                 send(
                     part.at[to], recv.at[source, slot], rs_send, rs_recv.at[source],
-                    (target, index(cx, to, core)),
+                    (target, along),
                 )
 
     whole_set = pl.ds(0, n_x * n_y)
     others = pl.ds(1, n_x * n_y - 1)
 
     def add_up(which, value):
-        for i in range(1, n_x * n_y):
-            value = value + recv[which, i]
-        return value
+        return pair_sum([value] + [recv[which, i] for i in range(1, n_x * n_y)])
 
     def reply(which, what, src, dst, grid, x):
         send(
@@ -172,8 +181,8 @@
         )
 
     def spread(i, src, ref):
-        for dy, c in column:
-            send(mine.at[src], ref.at[core, cy], ag_send.at[i], ag_recv.at[i], (g, index(cx, cy + dy, (core + c) % 2)))
+        for peer in gather_to:
+            send(mine.at[src], ref.at[core, cy], ag_send.at[i], ag_recv.at[i], (g, peer))
         ref[core, cy] = mine[src]
 
     @pl.when(z < n_z - 2)
@@ -223,6 +232,9 @@
 
     mine[SLOPE] = (mine[NEXT] - mine[PREVIOUS]) * 0.5
     spread(1, SLOPE, grad_ref)
+
+    wait_for(recv.at[FROM_OWN, others], ag_recv.at[0])
+    prepare(dens_ref, ready)
 
     @pl.when(first)
     def _():
@@ -249,54 +261,76 @@
 
     for i in range(2):
         wait_for(recv.at[FROM_OWN, others], ag_send.at[i])
-        wait_for(recv.at[FROM_OWN, others], ag_recv.at[i])
-
-
-def energy_kernel(dens_ref, grad_ref, dens_out, pot_out, flux_out):
-    rows, depth = dens_ref.shape[1:]
-    up, down = dens_ref[0], dens_ref[1]
-    dens_out[pl.ds(0, rows)] = up
-    dens_out[pl.ds(rows, rows)] = down
-    both = up + down
-    polar = (up - down) / both
+    wait_for(recv.at[FROM_OWN, others], ag_recv.at[1])
+    finish(grad_ref, ready, pot_ref, flux_ref)
+
+
+def prepare(dens_ref, ready):
+    rows, depth = ready.shape[2:]
+    pair = [dens_ref[i].reshape(rows, depth) for i in range(2)]
+    both = pair[0] + pair[1]
+    polar = (pair[0] - pair[1]) / both
     radius = radius_coef * jnp.exp(jnp.log(both) * (-1.0 / 3.0))
     inverse = 1.0 / (radius + 7.8)
     front = -0.44 * inverse
     even = (1.0 - 0.5 * polar * polar) * (1.0 + radius * inverse * (1.0 / 3.0))
-    for s, (value, sign) in enumerate(((up, 1.0), (down, -1.0))):
+    for i, (value, sign) in enumerate(zip(pair, (1.0, -1.0))):
         scaled = 2.0 * value
         cube = jnp.exp(jnp.log(scaled) * (1.0 / 3.0))
-        power = scaled * cube
-        over = 1.0 / power
+        over = 1.0 / (scaled * cube)
         grad_y = (pltpu.roll(value, rows - 1, 0) - pltpu.roll(value, 1, 0)) * 0.5
         grad_z = (pltpu.roll(value, depth - 1, 1) - pltpu.roll(value, 1, 1)) * 0.5
-        grad_x = grad_ref[s]
-        square = 4.0 * (grad_y * grad_y + grad_x * grad_x + grad_z * grad_z)
-        reduced = square * over * over * (1.0 / fermi_term)
+        unit = (4.0 / fermi_term) * over * over
+        terms = (
+            grad_y,
+            grad_z,
+            unit,
+            unit * (grad_y * grad_y + grad_z * grad_z),
+            -exchange_coef * cube,
+            front * (even - polar * (sign - polar)),
+            (-4.0 * exchange_coef * mu_value / fermi_term) * over,
+        )
+        for j, term in enumerate(terms):
+            ready[i, j] = term
+
+
+def finish(grad_ref, ready, pot_ref, flux_ref):
+    rows, depth = ready.shape[2:]
+    for i in range(2):
+        grad_x = grad_ref[i].reshape(rows, depth)
+        reduced = ready[i, 3] + ready[i, 2] * (grad_x * grad_x)
         ratio = 1.0 / (1.0 + (mu_value / kappa_value) * reduced)
         enhance = 1.0 + kappa_value - kappa_value * ratio
         slope = mu_value * ratio
-        exchange = -exchange_coef * cube * (
+        pot_ref[pl.ds(i * rows, rows)] = ready[i, 5] + ready[i, 4] * (
             (4.0 / 3.0) * enhance - (8.0 / 3.0) * (reduced * ratio) * slope
         )
-        pot_out[pl.ds(s * rows, rows)] = exchange + front * (even - polar * (sign - polar))
-        factor = (-4.0 * exchange_coef / fermi_term) * (slope * ratio) * over
-        for c, part in enumerate((grad_y, grad_x, grad_z)):
-            flux_out[pl.ds(s * 3 * rows + c, rows, stride=3)] = factor * part
+        factor = ready[i, 6] * (ratio * ratio)
+        for c, term in enumerate((ready[i, 0], grad_x, ready[i, 1])):
+            flux_ref[pl.ds(i * 3 * rows + c, rows, stride=3)] = factor * term
+
+
+def put_kernel(*refs):
+    sources, targets, sem = refs[:3], refs[3:6], refs[6]
+    copies = [pltpu.make_async_copy(a, b, sem.at[i]) for i, (a, b) in enumerate(zip(sources, targets))]
+    for copy in copies[::-1]:
+        copy.start()
+    for copy in copies:
+        copy.wait()
 
 
 def on_device(n_grid, n_x, n_y, n_z, orbitals, occupied, kweight):
     _, bands, rows, _, depth = orbitals.shape
     local = orbitals.reshape(bands, rows, depth)
     tile = rows // n_y
-    out = pltpu.VMEM((2, n_y, tile, depth), jnp.float32)
+    out = functools.partial(pltpu.VMEM, dtype=jnp.float32)
     vmem = pl.BlockSpec(memory_space=pltpu.VMEM)
     dma = pltpu.SemaphoreType.DMA
-    dens, grad = pl.pallas_call(
+    dens, pot, flux = pl.pallas_call(
         functools.partial(gather_kernel, (n_grid, n_x, n_y, n_z)),
-        out_shape=(out, out),
+        out_shape=(out((2, n_y, tile, depth)), out((2 * rows, depth)), out((6 * rows, depth))),
         in_specs=[pl.BlockSpec(memory_space=pl.ANY)] * 3,
-        out_specs=(vmem, vmem),
+        out_specs=(vmem,) * 3,
         scratch_shapes=[
             *[pltpu.VMEM((bands, rows // CHUNKS, depth), jnp.bfloat16) for _ in range(CHUNKS)],
             pltpu.SMEM(occupied.shape, jnp.int32),
@@ -304,7 +338,9 @@
             pltpu.VMEM((n_y, tile, depth), jnp.float32),
             pltpu.VMEM((3, 2 * n_y, tile, depth), jnp.float32),
             pltpu.VMEM((4, tile, depth), jnp.float32),
-            dma((CHUNKS,)),
+            pltpu.VMEM((2, n_y, tile, depth), jnp.float32),
+            pltpu.VMEM((2, 7, rows, depth), jnp.float32),
+            dma((CHUNKS * PARTS,)),
             dma((2,)),
             dma(()),
             dma((3,)),
@@ -319,16 +355,16 @@
         ),
         name="density",
     )(local, occupied, kweight)
-    dens, grad = dens.reshape(2, rows, depth), grad.reshape(2, rows, depth)
-    flat = functools.partial(jax.ShapeDtypeStruct, dtype=jnp.float32)
+    parts = (dens.reshape(2 * rows, depth), pot, flux)
     outs = pl.pallas_call(
-        energy_kernel,
-        out_shape=(flat((2 * rows, depth)), flat((2 * rows, depth)), flat((6 * rows, depth))),
-        in_specs=[vmem, vmem],
-        out_specs=(vmem, vmem, vmem),
+        put_kernel,
+        out_shape=[jax.ShapeDtypeStruct(part.shape, part.dtype) for part in parts],
+        in_specs=[vmem] * 3,
+        out_specs=[pl.BlockSpec(memory_space=pl.ANY)] * 3,
+        scratch_shapes=[dma((3,))],
         compiler_params=pltpu.CompilerParams(vmem_limit_bytes=8 << 20),
-        name="energy",
-    )(dens, grad)
+        name="put",
+    )(*parts)
     return (
         outs[0].reshape(2, rows, 1, depth),
         outs[1].reshape(2, rows, 1, depth),

time: 30.6 us -> 30.4 us (level)
  no operation moved by 1% of the time
where the time goes in v4:
time: 30.4 us; the launch traced here: 30.2 us
  Pallas kernels  29.6 us (97%)
  between operations  0.64 us (2%)
    pallas_call x1, Pallas kernels, on_device(): pl.pallas_call(functools.partial(gather_kernel, (n_grid, n_x, n_y, n_z)),...  28.9 us
    pallas_call x1, Pallas kernels, on_device(): pl.pallas_call(put_kernel, out_shape=[jax.ShapeDtypeStruct(part.shape, pa...  0.75 us

profile of v4, /device:TPU:1, one launch (start us, length us, event | category | flops | bytes accessed | tf_op | source)
XLA Modules:
  0.0 30.2 jit_solution(15681088589588549099)
XLA Ops:
  0.6 28.9 %density.1 = (f32[2,8,8,128]{3,2,1,0:T(8,128)S(1)}, f32[128,128]{1,0:T(8,128)S(1)}, f32[384,128]{1,0:T(8,128)S(1)}) custom-call(bf16[256,64,128]{2,1,0:T(8,128)(2,1)} %bitcast.10, s32[32]{0:T(128)} %occ_hbm.1, s32[32]{0:T(128)} %kw_hbm.1), custom_call_target="tpu_custom_call" | custom-call | tf_op jit(solution)/shard_map/density/pallas_call | solution.py:329
  29.5 0.7 %put.1 = (f32[128,128]{1,0:T(8,128)}, f32[128,128]{1,0:T(8,128)}, f32[384,128]{1,0:T(8,128)}) custom-call(f32[128,128]{1,0:T(8,128)S(1)} %bitcast.9, f32[128,128]{1,0:T(8,128)S(1)} %get-tuple-element.10.refs_1_, f32[384,128]{1,0:T(8,128)S(1)} %get-tuple-element.11.refs_2_), custom_call_target="tpu_custom_call" | custom-call | tf_op jit(solution)/shard_map/put/pallas_call | solution.py:359

commit v5 on v4

--- a/solution.py
+++ b/solution.py
@@ -70,7 +70,7 @@
 
     partner = index(cx, cy, 1 - core)
     column = [
-        (dy, c) for dy in sorted(range(n_y), key=lambda d: -min(d, n_y - d)) for c in range(2) if dy or c
+        (dy, c) for c in (1, 0) for dy in sorted(range(n_y), key=lambda d: -min(d, n_y - d)) if dy or c
     ]
     gather_to = [index(cx, cy + dy, lax.rem(core + c, 2)) for dy, c in column]
     rows_to = []

time: 30.4 us -> 30.3 us (level)
  no operation moved by 1% of the time
where the time goes in v5:
time: 30.3 us; the launch traced here: 30.2 us
  Pallas kernels  29.5 us (97%)
  between operations  0.64 us (2%)
    pallas_call x1, Pallas kernels, on_device(): pl.pallas_call(functools.partial(gather_kernel, (n_grid, n_x, n_y, n_z)),...  28.8 us
    pallas_call x1, Pallas kernels, on_device(): pl.pallas_call(put_kernel, out_shape=[jax.ShapeDtypeStruct(part.shape, pa...  0.75 us

profile of v5, /device:TPU:1, one launch (start us, length us, event | category | flops | bytes accessed | tf_op | source)
XLA Modules:
  0.0 30.2 jit_solution(2100396719396355781)
XLA Ops:
  0.6 28.8 %density.1 = (f32[2,8,8,128]{3,2,1,0:T(8,128)S(1)}, f32[128,128]{1,0:T(8,128)S(1)}, f32[384,128]{1,0:T(8,128)S(1)}) custom-call(bf16[256,64,128]{2,1,0:T(8,128)(2,1)} %bitcast.10, s32[32]{0:T(128)} %occ_hbm.1, s32[32]{0:T(128)} %kw_hbm.1), custom_call_target="tpu_custom_call" | custom-call | tf_op jit(solution)/shard_map/density/pallas_call | solution.py:329
  29.4 0.7 %put.1 = (f32[128,128]{1,0:T(8,128)}, f32[128,128]{1,0:T(8,128)}, f32[384,128]{1,0:T(8,128)}) custom-call(f32[128,128]{1,0:T(8,128)S(1)} %bitcast.9, f32[128,128]{1,0:T(8,128)S(1)} %get-tuple-element.10.refs_1_, f32[384,128]{1,0:T(8,128)S(1)} %get-tuple-element.11.refs_2_), custom_call_target="tpu_custom_call" | custom-call | tf_op jit(solution)/shard_map/put/pallas_call | solution.py:359
